TPU v7x, 512 devices: a whole 4x4x16 slice. The times are simulated.
512 devices in a mesh: freq: 32 (over z_lo, x), src: 2 (over z_hi), rcv: 8 (over y, core).
Axes of the slice: x: 4, y: 4, z: 16 (z_hi: 2, z_lo: 8; z = z_hi * 8 + z_lo), core: 2. Of those that a mesh axis runs over, the one named last changes fastest.
Arguments:
- traces: float32 [1024, 1024, 256], P(('src', 'freq'), 'rcv'), may hold values from -6 to 6
Outputs:
- multiples: float32 [2, 96, 1024, 1024], P(None, 'freq', 'src', 'rcv')
All inputs are finite; a program needn't handle non-finite values.
Results may differ from a plain program's by a relative error of at most 0.000098.
Values sent between devices are 32-bit elements; how exact they have to be, the bound alone decides.
A program may use at most 64 MiB of HBM per device.

v0:
```python
import math

import jax
import jax.numpy as jnp
from jax import lax
from jax.sharding import PartitionSpec as P

N = 1024
FPD = 3


def dft_matrix(n_time, n_freq):
    times = jnp.arange(n_time, dtype=jnp.int32)
    bins = jnp.arange(n_freq, dtype=jnp.int32)
    phase = times[:, None] * bins[None, :] % n_time
    angle = phase.astype(jnp.float32) * (2.0 * math.pi / n_time)
    both = jnp.stack([jnp.cos(angle), -jnp.sin(angle)], axis=-1)
    return both.reshape(n_time, 2 * n_freq) * (1.0 / math.sqrt(n_time))


def batched_dot(left, right):
    return jnp.einsum(
        "mgq,mqn->mgn",
        left,
        right,
        precision=lax.Precision.HIGHEST,
        preferred_element_type=jnp.float32,
    )


def complex_product(left_re, left_im, right_re, right_im):
    real_part = batched_dot(left_re, right_re) - batched_dot(left_im, right_im)
    imag_part = batched_dot(left_re, right_im) + batched_dot(left_im, right_re)
    return (real_part, imag_part)


def per_device(traces):
    n_time = traces.shape[2]
    n_freq = FPD * lax.axis_size("freq")
    dft_table = dft_matrix(n_time, n_freq)
    spectra = jnp.einsum(
        "srt,tk->ksr",
        traces,
        dft_table,
        precision=lax.Precision.HIGHEST,
        preferred_element_type=jnp.float32,
    )
    regrouped = lax.all_to_all(spectra, "freq", split_axis=0, concat_axis=1, tiled=True)
    src_rows = regrouped.shape[1]
    rcv_cols = regrouped.shape[2]
    split_parts = regrouped.reshape(FPD, 2, src_rows, rcv_cols)
    local_re = split_parts[:, 0]
    local_im = split_parts[:, 1]
    col_re, col_im = (
        lax.all_gather(local_re, "src", axis=1, tiled=True),
        lax.all_gather(local_im, "src", axis=1, tiled=True),
    )
    piece_re = lax.all_gather(local_re, "rcv", axis=2, tiled=True)
    piece_im = lax.all_gather(local_im, "rcv", axis=2, tiled=True)
    real_part, imag_part = complex_product(piece_re, piece_im, col_re, col_im)
    scale = -1.0 / math.sqrt(N)
    return jnp.stack([real_part, imag_part]) * scale


def solution(mesh):
    in_specs = (P(("src", "freq"), "rcv", None),)
    out_specs = P(None, "freq", "src", "rcv")
    return jax.shard_map(
        per_device, mesh=mesh, in_specs=in_specs, out_specs=out_specs, check_vma=False
    )
```

profile of v0, /device:TPU:1, one launch (start us, length us, event | category | flops | bytes accessed | tf_op | source)
XLA Modules:
  0.0 411.7 jit_solution(3908307167513742405)
XLA Ops:
  6.5 0.0 copy-start
  6.5 0.0 all-gather.11.cloned.1.call-start
  6.5 0.4 sine_negate_fusion
  7.0 0.2 copy.14
  7.1 0.1 reshape.83
  7.3 0.8 copy-done
  8.1 2.3 fusion.39
  10.4 0.9 copy.15
  11.3 89.4 %all_to_all.15 = f32[192,16,128]{2,1,0:T(8,128)S(1)} all-to-all(f32[192,16,128]{2,1,0:T(8,128)S(1)} %copy.15), channel_id=1, replica_groups=mesh['freq'=32,'src'=2,'rcv'=8] {'freq'}, dimensions={0} | all-to-all | bytes 3145728 | tf_op jit(solution)/shard_map/all_to_all | solution.py:48
  100.7 0.1 copy.16
  100.9 1.3 slice_bitcast_fusion.1
  102.1 0.0 all-gather.11.cloned.1.call-update
  102.1 0.0 all-gather.13.cloned.1.call-start
  102.2 0.7 all-gather.13.cloned.1.call-update
  102.9 0.0 all-gather.15.cloned.1.call-start
  102.9 0.7 all-gather.15.cloned.1.call-update
  103.6 0.2 all-gather.9.cloned.1.call-start
  103.9 0.3 all-gather.9.cloned.1.call-update
  104.2 90.4 %all-gather.11.cloned.1.call-done = f32[3,1,1024,128]{3,2,0,1:T(8,128)} async-done(((f32[3,1,512,128]{3,2,0,1:T(8,128)}), f32[3,1,1024,128]{3,2,0,1:T(8,128)}) %all-gather.11.cloned.1.call-update) | async-done | bytes 1572880 | tf_op jit(solution)/shard_map/all_gather | solution.py:55
  194.6 48.8 %all-gather.13.cloned.1.call-done = f32[3,1,512,1024]{3,2,0,1:T(8,128)} async-done(((f32[3,1,512,128]{3,2,0,1:T(8,128)}), f32[3,1,512,1024]{3,2,0,1:T(8,128)}) %all-gather.13.cloned.1.call-update) | async-done | bytes 6291472 | tf_op jit(solution)/shard_map/all_gather | solution.py:59
  243.4 7.9 %fusion = f32[3,512,128]{2,1,0:T(8,128)S(1)} fusion(f32[3,1,512,1024]{3,2,0,1:T(8,128)} %all-gather.13.cloned.1.call-done, f32[3,1,1024,128]{3,2,0,1:T(8,128)} %all-gather.11.cloned.1.call-done), kind=kOutput, calls=%fused_computation | convolution fusion | flops 2415919104 | bytes 8650752 | tf_op jit(solution)/shard_map/mgq,mqn->mgn/dot_general | solution.py:22
  251.3 90.1 %all-gather.15.cloned.1.call-done = f32[3,1,1024,128]{3,2,0,1:T(8,128)} async-done(((f32[3,1,512,128]{3,2,0,1:T(8,128)}), f32[3,1,1024,128]{3,2,0,1:T(8,128)}) %all-gather.15.cloned.1.call-update) | async-done | bytes 1572880 | tf_op jit(solution)/shard_map/all_gather | solution.py:56
  341.4 8.8 %fusion.2 = f32[3,512,128]{2,1,0:T(8,128)} fusion(f32[3,1,512,1024]{3,2,0,1:T(8,128)} %all-gather.13.cloned.1.call-done, f32[3,1,1024,128]{3,2,0,1:T(8,128)} %all-gather.15.cloned.1.call-done), kind=kOutput, calls=%fused_computation.2 | convolution fusion | flops 2415919104 | bytes 8650752 | tf_op jit(solution)/shard_map/mgq,mqn->mgn/dot_general | solution.py:22
  350.2 39.8 %all-gather.9.cloned.1.call-done = f32[3,1,512,1024]{3,2,0,1:T(8,128)} async-done(((f32[3,1,512,128]{3,2,0,1:T(8,128)}), f32[3,1,512,1024]{3,2,0,1:T(8,128)}) %all-gather.9.cloned.1.call-update) | async-done | bytes 6291472 | tf_op jit(solution)/shard_map/all_gather | solution.py:58
  390.1 0.0 copy-start.1
  390.1 0.0 copy-start.3
  390.1 8.4 %fusion.22 = f32[1,3,512,128]{3,2,1,0:T(8,128)S(1)} fusion(f32[3,512,128]{2,1,0:T(8,128)S(1)} %fusion, f32[3,1,1024,128]{3,2,0,1:T(8,128)} %all-gather.15.cloned.1.call-done, f32[3,1,512,1024]{3,2,0,1:T(8,128)} %all-gather.9.cloned.1.call-done), kind=kOutput, calls=%fused_computation.15 | convolution fusion | flops 2416115712 | bytes 9437184 | tf_op jit(solution)/shard_map/mgq,mqn->mgn/dot_general | solution.py:22
  398.5 0.0 copy-done.1
  398.5 0.0 copy-done.2
  398.5 0.0 copy-done.3
  398.5 5.4 %fusion.27 = f32[1,3,512,128]{3,2,1,0:T(8,128)S(1)} fusion(f32[3,512,128]{2,1,0:T(8,128)S(1)} %copy-done.3, f32[3,1,1024,128]{3,2,0,1:T(8,128)S(1)} %copy-done.2, f32[3,1,512,1024]{3,2,0,1:T(8,128)S(1)} %copy-done.1), kind=kOutput, calls=%fused_computation.16 | convolution fusion | flops 2416115712 | bytes 9437184 | tf_op jit(solution)/shard_map/mgq,mqn->mgn/dot_general | solution.py:22
  403.9 1.2 maximum_multiply_fusion
  (2 shorter events, 0.0 us)
Async XLA Ops:
  6.5 1.6 copy-start
  6.5 188.0 %all-gather.11.cloned.1.call-start = ((), (), s32[]{:S(2)}) async-start(), calls=%async_computation.2 | async-start | bytes 2359296 | tf_op jit(solution)/shard_map/all_gather | solution.py:55
  102.1 141.2 %all-gather.13.cloned.1.call-start = ((), (), s32[]{:S(2)}) async-start(), calls=%async_computation.3 | async-start | bytes 7077888 | tf_op jit(solution)/shard_map/all_gather | solution.py:59
  102.9 238.5 %all-gather.15.cloned.1.call-start = ((), (), s32[]{:S(2)}) async-start(), calls=%async_computation.4 | async-start | bytes 2359296 | tf_op jit(solution)/shard_map/all_gather | solution.py:56
  103.6 286.5 %all-gather.9.cloned.1.call-start = ((), (), s32[]{:S(2)}) async-start(), calls=%async_computation.1 | async-start | bytes 7077888 | tf_op jit(solution)/shard_map/all_gather | solution.py:58
  390.1 8.4 %copy-start.1 = (f32[3,1,512,1024]{3,2,0,1:T(8,128)S(1)}, f32[3,1,512,1024]{3,2,0,1:T(8,128)}, u32[]{:S(2)}) copy-start(f32[3,1,512,1024]{3,2,0,1:T(8,128)} %all-gather.9.cloned.1.call-done) | copy-start | bytes 18874372
  390.1 8.4 %copy-start.2 = (f32[3,1,1024,128]{3,2,0,1:T(8,128)S(1)}, f32[3,1,1024,128]{3,2,0,1:T(8,128)}, u32[]{:S(2)}) copy-start(f32[3,1,1024,128]{3,2,0,1:T(8,128)} %all-gather.11.cloned.1.call-done) | copy-start | bytes 4718596
  390.1 8.4 %copy-start.3 = (f32[3,512,128]{2,1,0:T(8,128)S(1)}, f32[3,512,128]{2,1,0:T(8,128)}, u32[]{:S(2)}) copy-start(f32[3,512,128]{2,1,0:T(8,128)} %fusion.2) | copy-start | bytes 2359300
Sparse Core Ops, SparseCore 0:
  102.3 92.2 all-gather.10
  196.7 46.6 all-gather.12
  245.5 95.8 all-gather.14
  343.4 46.6 all-gather.8
where the time goes:
time: 412 us
  waiting for transfers between devices  271 us (66%)
  blocking collectives  89.4 us (22%)
  matrix products  32.8 us (8%)
  between operations  13.2 us (3%)
    all_gather x1, waiting for transfers between devices, per_device(): lax.all_gather(local_re, 'src', axis=1, tiled=True)  90.4 us
    all_gather x1, waiting for transfers between devices, per_device(): lax.all_gather(local_im, 'src', axis=1, tiled=True)  90.1 us
    all_to_all x1, blocking collectives, per_device(): lax.all_to_all(spectra, 'freq', split_axis=0, concat_axis=1, tiled=True)  89.4 us
    all_gather x1, waiting for transfers between devices, per_device(): piece_im = lax.all_gather(local_im, 'rcv', axis=2, tiled=True)  48.8 us
    all_gather x1, waiting for transfers between devices, per_device(): piece_re = lax.all_gather(local_re, 'rcv', axis=2, tiled=True)  39.8 us
    dot_general x4, matrix products, batched_dot(): jnp.einsum('mgq,mqn->mgn', left, right, precision=lax.Precision.HIGHEST,...  30.5 us
  transfers between devices with their start and end apart: 4, of which 4 were waited for; matrix products, arithmetic and copies ran while one was open for 4% of the time, Pallas kernels for 0%

commit v1 on v0

v1 whole, which is shorter than its diff:
```python
import math

import jax
import jax.numpy as jnp
import ml_dtypes
import numpy as np
from jax import lax
from jax.experimental import pallas as pl
from jax.experimental.pallas import tpu as pltpu
from jax.sharding import PartitionSpec as P

N = 1024
NT = 256
NF = 96
FPD = 3
PLANES = 2 * FPD
BLOCK = 16 * PLANES
GROUP = 4 * BLOCK
HALF = 8 * GROUP
ROW = 2 * HALF
MESH = pl.DeviceIdType.MESH
SCALE = -1.0 / math.sqrt(N)
ORDER = [(0, i) for i in range(1, 8)] + [(1, i) for i in range(1, 9)]
XPART = 4


def split(x):
    hi = x.astype(jnp.bfloat16)
    return hi, (x - hi.astype(jnp.float32)).astype(jnp.bfloat16)


def dft_table():
    phase = np.arange(NF)[:, None] * np.arange(NT)[None, :] % NT
    angle = phase * (2.0 * math.pi / NT)
    both = np.stack([np.cos(angle), -np.sin(angle)], axis=1)
    both = (both.reshape(2 * NF, NT) / math.sqrt(NT)).astype(np.float32)
    hi = both.astype(ml_dtypes.bfloat16)
    lo = (both - hi.astype(np.float32)).astype(ml_dtypes.bfloat16)
    return np.stack([hi, lo])


def near(i, at, count):
    sides = jnp.minimum(at, count - 1 - at)
    both = i <= 2 * sides
    far = jnp.where(both, (i + 1) // 2, i - sides)
    up = jnp.where(both, i % 2 == 1, at < count // 2)
    return jnp.where(up, far, -far)


def across(i, at):
    if i == 8:
        return 8
    up_first, down_first = 8 - at, at + 1
    single = jnp.abs(2 * at - 7)
    one = i <= single
    j = i - single
    far = jnp.where(
        one,
        jnp.minimum(up_first, down_first) + i - 1,
        jnp.maximum(up_first, down_first) + (j - 1) // 2,
    )
    up = jnp.where(one, at >= 4, j % 2 == 1)
    return jnp.where(up, far, -far)


def kernel(
    traces,
    table,
    out,
    xin,
    spec,
    big,
    ahi,
    alo,
    bhi,
    blo,
    xsem,
    lsem,
    zsend,
    ysend,
    csend,
    zsem,
    ysem,
    csem,
):
    f = lax.axis_index("freq")
    h = lax.axis_index("src")
    r = lax.axis_index("rcv")
    x, zl = lax.rem(f, 4), f // 4
    y, c = r // 2, lax.rem(r, 2)
    z = h * 8 + zl

    def device(dx, dy, dz, dc):
        x2, y2 = lax.rem(x + dx, 4), lax.rem(y + dy, 4)
        z2, c2 = lax.rem(z + dz + 16, 16), lax.rem(c + dc, 2)
        return (lax.rem(z2, 8) * 4 + x2, z2 // 8, y2 * 2 + c2)

    def rows(start, n):
        return big.at[pl.ds(pl.multiple_of(start, BLOCK), n)]

    def wait(ref, sem):
        pltpu.make_async_copy(ref, ref, sem).wait()

    def send(src, dst, ssem, rsem, to):
        pltpu.make_async_remote_copy(
            src, dst, ssem, rsem, device_id=to, device_id_type=MESH
        ).start()

    barrier = pltpu.get_barrier_semaphore()
    peers = [(dx, 0, dz, 0) for dz in range(16) for dx in range(4) if dx or dz]
    peers += [(0, dy, 0, 0) for dy in (1, 2, 3)] + [(0, 0, 0, 1)]
    per = 2048 // XPART
    loads = [
        pltpu.make_async_copy(
            traces.at[pl.ds(k * per, per)], xin.at[pl.ds(k * per, per)], xsem.at[k]
        )
        for k in range(XPART)
    ]
    with jax.named_scope("signal"):
        for load in loads:
            load.start()
        for p in peers:
            pl.semaphore_signal(
                barrier, inc=1, device_id=device(*p), device_id_type=MESH
            )
    with jax.named_scope("dft"):
        thi, tlo = table[0], table[1]
        dims = (((1,), (1,)), ((), ()))
        for k in range(8):
            if k % (8 // XPART) == 0:
                loads[k // (8 // XPART)].wait()
            xhi, xlo = split(xin[pl.ds(k * 256, 256), :])
            got = sum(
                lax.dot_general(a, b, dims, preferred_element_type=jnp.float32)
                for a, b in ((thi, xhi), (tlo, xhi), (thi, xlo))
            )
            for i in range(2):
                spec[pl.ds(2 * k + i, 2 * NF, stride=16), :] = got[
                    :, i * 128 : (i + 1) * 128
                ]
    with jax.named_scope("barrier"):
        pl.semaphore_wait(barrier, len(peers))

    with jax.named_scope("issue"):
        mine = (z * 4 + x) * BLOCK

        def zcopy(dz, dx):
            to = device(dx, 0, dz, 0)
            src = spec.at[pl.ds(pl.multiple_of(to[0] * BLOCK, BLOCK), BLOCK)]
            send(src, rows(mine, BLOCK), zsend, zsem.at[z], to)

        own = pltpu.make_async_copy(
            spec.at[pl.ds(pl.multiple_of(f * BLOCK, BLOCK), BLOCK)],
            rows(mine, BLOCK),
            lsem,
        )
        own.start()
        for dx in (1, 2, 3):
            zcopy(0, dx)
        for kind, i in ORDER:
            dz = across(i, zl) if kind else near(i, zl, 8)
            for dx in range(4):
                zcopy(dz, dx)
        own.wait()

    def place(i):
        return zl + (near(i, zl, 8) if i else 0)

    def pass_on(i):
        at = place(i)
        for dy in (1, 3, 2):
            q = lax.rem(y - dy + 4, 4) * 2 + c
            ref = rows(ROW + q * HALF + at * GROUP, GROUP)
            wait(ref, ysem.at[(dy - 1) * 8 + at])
            send(ref, ref, csend, csem.at[dy * 8 + at], device(0, 0, 0, 1))

    for i in range(8):
        at = place(i)
        src = rows((h * 8 + at) * GROUP, GROUP)
        dst = rows(ROW + r * HALF + at * GROUP, GROUP)
        with jax.named_scope(f"own{i}"):
            wait(
                rows((h * 8 + at) * GROUP, GROUP if i else GROUP - BLOCK),
                zsem.at[h * 8 + at],
            )
        with jax.named_scope(f"fwd{i}"):
            for dy in (1, 3, 2):
                send(src, dst, ysend, ysem.at[(dy - 1) * 8 + at], device(0, dy, 0, 0))
            send(src, dst, csend, csem.at[at], device(0, 0, 0, 1))
        if i:
            with jax.named_scope(f"pass{i - 1}"):
                pass_on(i - 1)
    with jax.named_scope("pass7"):
        pass_on(7)
    with jax.named_scope("core"):
        for dy in range(4):
            q = lax.rem(y - dy + 4, 4) * 2 + 1 - c
            for at in range(8):
                wait(rows(ROW + q * HALF + at * GROUP, GROUP), csem.at[dy * 8 + at])

    def load(start):
        return big[pl.ds(pl.multiple_of(start, 16), 16), :]

    def chunk(q, first):
        base = jnp.where(q == r, h * HALF, ROW + q * HALF)

        def left(g, carry):
            at = pl.ds(pl.multiple_of(g * 16, 16), 16)
            for k in range(FPD):
                for part in range(2):
                    hi, lo = split(load(base + g * BLOCK + (2 * k + part) * 16))
                    lanes = pl.ds(part * 128, 128)
                    ahi[k, at, lanes] = hi
                    alo[k, at, lanes] = lo
            return carry

        lax.fori_loop(0, 32, left, 0)
        for b in range(8):
            for k in range(FPD):
                start = (q * 8 + b) * BLOCK + 2 * k * 16
                for part in range(2):
                    value = load(start + part * 16) * SCALE
                    for ref, v in zip((bhi, blo), split(value)):
                        ref[k, pl.ds(part * 128 + b * 16, 16), pl.ds(0, 128)] = (
                            v if part == 0 else -v
                        )
                        ref[k, pl.ds((1 - part) * 128 + b * 16, 16), pl.ds(128, 128)] = v
        return first

    def multiply(first):
        for k in range(FPD):
            for m in range(2):
                at = pl.ds(m * 256, 256)
                got = sum(
                    jnp.dot(a[k, at, :], b[k], preferred_element_type=jnp.float32)
                    for a, b in ((ahi, bhi), (alo, bhi), (ahi, blo))
                )
                for part in range(2):
                    piece = got[:, part * 128 : (part + 1) * 128]
                    if first:
                        out[part, k, at, :] = piece
                    else:
                        out[part, k, at, :] += piece

    for i in range(4):
        with jax.named_scope(f"near{i}"):
            chunk(h * 4 + i, i == 0)
            multiply(i == 0)
    mid = zl // 2
    for i in range(3, -1, -1):
        q = (1 - h) * 4 + mid + (near(i, mid, 4) if i else 0)
        with jax.named_scope(f"wait{i}"):
            for k in range(2):
                wait(rows((2 * q + k) * GROUP, GROUP), zsem.at[2 * q + k])
        with jax.named_scope(f"far{i}"):
            chunk(q, False)
            multiply(False)
    with jax.named_scope("end"):
        wait(big.at[pl.ds(0, 63 * BLOCK)], zsend)
        wait(big.at[pl.ds(0, 3 * HALF)], ysend)
        wait(big.at[pl.ds(0, 4 * HALF)], csend)


def per_device(traces):
    table = jnp.asarray(dft_table())
    vmem = pl.BlockSpec(memory_space=pltpu.VMEM)
    dma = pltpu.SemaphoreType.DMA
    return pl.pallas_call(
        kernel,
        name="multiples",
        out_shape=jax.ShapeDtypeStruct((2, FPD, N // 2, 128), jnp.float32),
        in_specs=[pl.BlockSpec(memory_space=pltpu.HBM), vmem],
        out_specs=vmem,
        scratch_shapes=[
            pltpu.VMEM((2048, NT), jnp.float32),
            pltpu.VMEM((2 * NF * 16, 128), jnp.float32),
            pltpu.VMEM((ROW + 8 * HALF, 128), jnp.float32),
            pltpu.VMEM((FPD, 512, 256), jnp.bfloat16),
            pltpu.VMEM((FPD, 512, 256), jnp.bfloat16),
            pltpu.VMEM((FPD, 256, 256), jnp.bfloat16),
            pltpu.VMEM((FPD, 256, 256), jnp.bfloat16),
            dma((XPART,)),
            dma,
            dma,
            dma,
            dma,
            dma((16,)),
            dma((24,)),
            dma((32,)),
        ],
        compiler_params=pltpu.CompilerParams(
            collective_id=0, has_side_effects=True, vmem_limit_bytes=40 << 20
        ),
    )(traces.reshape(2048, NT), table)


def solution(mesh):
    in_specs = (P(("src", "freq"), "rcv", None),)
    out_specs = P(None, "freq", "src", "rcv")
    return jax.shard_map(
        per_device, mesh=mesh, in_specs=in_specs, out_specs=out_specs, check_vma=False
    )
```

time: 412 us -> 165 us (0.40)
  waiting for transfers between devices: 271 us -> 0 us
  Pallas kernels: 0 us -> 161 us
  blocking collectives: 89.4 us -> 0 us
  matrix products: 32.8 us -> 0 us
  between operations: 13.2 us -> 0.01 us
    all_gather x4 -> x0, waiting for transfers between devices: 269 us -> none  [the longest x1 90.4 us: per_device(): lax.all_gather(local_re, 'src', axis=1, tiled=True)]
    pallas_call x0 -> x1, Pallas kernels: none -> 161 us  [per_device(): pl.pallas_call(kernel, name='multiples', out_shape=jax.ShapeDtypeStruct((...]
    all_to_all x1 -> x0, blocking collectives: 89.4 us -> none  [per_device(): lax.all_to_all(spectra, 'freq', split_axis=0, concat_axis=1, tiled=True)]
    dot_general x5 -> x0, matrix products: 32.8 us -> none  [the longest x4 30.5 us: batched_dot(): jnp.einsum('mgq,mqn->mgn', left, right, precision=lax.Precision.HIGHEST,...]
  transfers between devices with their start and end apart: 4 -> 0, of which waited for: 4 -> 0; matrix products, arithmetic and copies ran while one was open for 4% -> 0% of each run, Pallas kernels for 0% -> 0%
where the time goes in v1:
time: 165 us
  Pallas kernels  161 us (98%)
  local copies, waits for them, and re-layouts  3.66 us (2%)
    pallas_call x1, Pallas kernels, per_device(): pl.pallas_call(kernel, name='multiples', out_shape=jax.ShapeDtypeStruct((...  161 us
    unnamed x5, local copies, waits for them, and re-layouts  3.66 us

profile of v1, /device:TPU:1, one launch (start us, length us, event | category | flops | bytes accessed | tf_op | source)
XLA Modules:
  0.0 164.7 jit_solution(5630545404707000188)
XLA Ops:
  0.0 0.0 copy-start
  0.0 1.6 copy-done
  1.6 0.0 copy-start.1
  1.6 0.9 copy-done.1
  2.5 161.0 %multiples.1 = f32[2,3,512,128]{3,2,1,0:T(8,128)S(1)} custom-call(f32[2048,256]{1,0:T(8,128)S(1)} %bitcast.1, bf16[2,192,256]{2,1,0:T(8,128)(2,1)S(1)} %copy-done.1), custom_call_target="tpu_custom_call" | custom-call | tf_op jit(solution)/shard_map/multiples/pallas_call | solution.py:268
  163.6 1.1 copy.4
Async XLA Ops:
  0.0 1.6 copy-start
  1.6 0.9 copy-start.1

commit v2 on v1

--- a/solution.py
+++ b/solution.py
@@ -1,3 +1,4 @@
+import functools
 import math
 
 import jax
@@ -20,8 +21,8 @@
 ROW = 2 * HALF
 MESH = pl.DeviceIdType.MESH
 SCALE = -1.0 / math.sqrt(N)
-ORDER = [(0, i) for i in range(1, 8)] + [(1, i) for i in range(1, 9)]
 XPART = 4
+RFIRST = 6
 
 
 def split(x):
@@ -47,33 +48,22 @@
     return jnp.where(up, far, -far)
 
 
-def across(i, at):
-    if i == 8:
-        return 8
-    up_first, down_first = 8 - at, at + 1
-    single = jnp.abs(2 * at - 7)
-    one = i <= single
-    j = i - single
-    far = jnp.where(
-        one,
-        jnp.minimum(up_first, down_first) + i - 1,
-        jnp.maximum(up_first, down_first) + (j - 1) // 2,
-    )
-    up = jnp.where(one, at >= 4, j % 2 == 1)
-    return jnp.where(up, far, -far)
-
-
 def kernel(
     traces,
     table,
     out,
     xin,
+    tab,
     spec,
     big,
     ahi,
     alo,
     bhi,
     blo,
+    whi,
+    wlo,
+    nhi,
+    nlo,
     xsem,
     lsem,
     zsend,
@@ -82,6 +72,10 @@
     zsem,
     ysem,
     csem,
+    ready,
+    relay,
+    rsem,
+    rsend,
 ):
     f = lax.axis_index("freq")
     h = lax.axis_index("src")
@@ -107,7 +101,7 @@
         ).start()
 
     barrier = pltpu.get_barrier_semaphore()
-    peers = [(dx, 0, dz, 0) for dz in range(16) for dx in range(4) if dx or dz]
+    peers = [(dx, 0, dz, 0) for dz in (1, -1, 0) for dx in range(4) if dx or dz]
     peers += [(0, dy, 0, 0) for dy in (1, 2, 3)] + [(0, 0, 0, 1)]
     per = 2048 // XPART
     loads = [
@@ -116,15 +110,17 @@
         )
         for k in range(XPART)
     ]
+    loads.append(pltpu.make_async_copy(table, tab, xsem.at[XPART]))
     with jax.named_scope("signal"):
-        for load in loads:
-            load.start()
         for p in peers:
             pl.semaphore_signal(
                 barrier, inc=1, device_id=device(*p), device_id_type=MESH
             )
+        for load in loads[-1:] + loads[:-1]:
+            load.start()
     with jax.named_scope("dft"):
-        thi, tlo = table[0], table[1]
+        loads[XPART].wait()
+        thi, tlo = tab[0], tab[1]
         dims = (((1,), (1,)), ((), ()))
         for k in range(8):
             if k % (8 // XPART) == 0:
@@ -144,10 +140,15 @@
     with jax.named_scope("issue"):
         mine = (z * 4 + x) * BLOCK
 
+        def flag(to):
+            at = to[0] // 4
+            farthest = zl == jnp.where(at < 4, 7, 0)
+            return jnp.where((to[1] == h) & farthest, 16 + x, z)
+
         def zcopy(dz, dx):
             to = device(dx, 0, dz, 0)
             src = spec.at[pl.ds(pl.multiple_of(to[0] * BLOCK, BLOCK), BLOCK)]
-            send(src, rows(mine, BLOCK), zsend, zsem.at[z], to)
+            send(src, rows(mine, BLOCK), zsend, zsem.at[flag(to)], to)
 
         own = pltpu.make_async_copy(
             spec.at[pl.ds(pl.multiple_of(f * BLOCK, BLOCK), BLOCK)],
@@ -157,11 +158,49 @@
         own.start()
         for dx in (1, 2, 3):
             zcopy(0, dx)
-        for kind, i in ORDER:
-            dz = across(i, zl) if kind else near(i, zl, 8)
-            for dx in range(4):
-                zcopy(dz, dx)
-        own.wait()
+
+    def spread(dz):
+        for dx in range(4):
+            zcopy(dz, dx)
+
+    def via(dx):
+        return 4 if dx < 2 else -4
+
+    def halfway(dx):
+        to = device(dx, 0, via(dx), 0)
+        goal = device(dx, 0, 8, 0)[0]
+        src = spec.at[pl.ds(pl.multiple_of(goal * BLOCK, BLOCK), BLOCK)]
+        slot = relay.at[pl.ds(dx * BLOCK, BLOCK)]
+        send(src, slot, zsend, rsem.at[dx // 2], to)
+
+    def onward(dx):
+        to = device(0, 0, via(dx), 0)
+        first = lax.rem(z - via(dx) + 16, 16)
+        block = (first * 4 + lax.rem(x - dx + 4, 4)) * BLOCK
+        slot = relay.at[pl.ds(dx * BLOCK, BLOCK)]
+        send(slot, rows(block, BLOCK), rsend, zsem.at[first], to)
+
+    for k in range(1, 8):
+        with jax.named_scope(f"ready{k}"):
+            for s in range(2):
+                if k > 1:
+                    pl.semaphore_wait(ready.at[s, k], 1)
+                if k < 7:
+                    pl.semaphore_signal(
+                        ready.at[s, k + 1],
+                        inc=1,
+                        device_id=device(0, 0, 2 * s - 1, 0),
+                        device_id_type=MESH,
+                    )
+            if k == RFIRST:
+                for dx in range(4):
+                    halfway(dx)
+            spread(k)
+            spread(-k)
+    if RFIRST == 8:
+        for dx in range(4):
+            halfway(dx)
+    own.wait()
 
     def place(i):
         return zl + (near(i, zl, 8) if i else 0)
@@ -174,7 +213,7 @@
             wait(ref, ysem.at[(dy - 1) * 8 + at])
             send(ref, ref, csend, csem.at[dy * 8 + at], device(0, 0, 0, 1))
 
-    for i in range(8):
+    def take(i):
         at = place(i)
         src = rows((h * 8 + at) * GROUP, GROUP)
         dst = rows(ROW + r * HALF + at * GROUP, GROUP)
@@ -183,28 +222,24 @@
                 rows((h * 8 + at) * GROUP, GROUP if i else GROUP - BLOCK),
                 zsem.at[h * 8 + at],
             )
-        with jax.named_scope(f"fwd{i}"):
-            for dy in (1, 3, 2):
-                send(src, dst, ysend, ysem.at[(dy - 1) * 8 + at], device(0, dy, 0, 0))
-            send(src, dst, csend, csem.at[at], device(0, 0, 0, 1))
-        if i:
-            with jax.named_scope(f"pass{i - 1}"):
-                pass_on(i - 1)
-    with jax.named_scope("pass7"):
-        pass_on(7)
-    with jax.named_scope("core"):
+        for dy in (1, 3, 2):
+            send(src, dst, ysend, ysem.at[(dy - 1) * 8 + at], device(0, dy, 0, 0))
+        send(src, dst, csend, csem.at[at], device(0, 0, 0, 1))
+
+    def from_core(i):
+        at = place(i)
         for dy in range(4):
             q = lax.rem(y - dy + 4, 4) * 2 + 1 - c
-            for at in range(8):
-                wait(rows(ROW + q * HALF + at * GROUP, GROUP), csem.at[dy * 8 + at])
+            wait(rows(ROW + q * HALF + at * GROUP, GROUP), csem.at[dy * 8 + at])
 
     def load(start):
         return big[pl.ds(pl.multiple_of(start, 16), 16), :]
 
-    def chunk(q, first):
+    def left(q, g0, n, ahi, alo):
         base = jnp.where(q == r, h * HALF, ROW + q * HALF)
 
-        def left(g, carry):
+        def one(j, carry):
+            g = g0 + j
             at = pl.ds(pl.multiple_of(g * 16, 16), 16)
             for k in range(FPD):
                 for part in range(2):
@@ -214,25 +249,29 @@
                     alo[k, at, lanes] = lo
             return carry
 
-        lax.fori_loop(0, 32, left, 0)
+        lax.fori_loop(0, n, one, 0)
+
+    def right(q, slot, bhi, blo):
         for b in range(8):
             for k in range(FPD):
                 start = (q * 8 + b) * BLOCK + 2 * k * 16
                 for part in range(2):
                     value = load(start + part * 16) * SCALE
                     for ref, v in zip((bhi, blo), split(value)):
-                        ref[k, pl.ds(part * 128 + b * 16, 16), pl.ds(0, 128)] = (
+                        i = slot * FPD + k
+                        ref[i, pl.ds(part * 128 + b * 16, 16), pl.ds(0, 128)] = (
                             v if part == 0 else -v
                         )
-                        ref[k, pl.ds((1 - part) * 128 + b * 16, 16), pl.ds(128, 128)] = v
-        return first
-
-    def multiply(first):
+                        ref[i, pl.ds((1 - part) * 128 + b * 16, 16), pl.ds(128, 128)] = v
+
+    def multiply(slot, row0, sizes, ahi, alo, bhi, blo, first=False):
         for k in range(FPD):
-            for m in range(2):
-                at = pl.ds(m * 256, 256)
+            row = row0
+            for size in sizes:
+                at = pl.ds(row if isinstance(row, int) else pl.multiple_of(row, 32), size)
+                i = slot * FPD + k
                 got = sum(
-                    jnp.dot(a[k, at, :], b[k], preferred_element_type=jnp.float32)
+                    jnp.dot(a[k, at, :], b[i], preferred_element_type=jnp.float32)
                     for a, b in ((ahi, bhi), (alo, bhi), (ahi, blo))
                 )
                 for part in range(2):
@@ -241,22 +280,103 @@
                         out[part, k, at, :] = piece
                     else:
                         out[part, k, at, :] += piece
-
-    for i in range(4):
-        with jax.named_scope(f"near{i}"):
-            chunk(h * 4 + i, i == 0)
-            multiply(i == 0)
+                row = row + size
+
     mid = zl // 2
-    for i in range(3, -1, -1):
-        q = (1 - h) * 4 + mid + (near(i, mid, 4) if i else 0)
+    swap = (zl == 2) | (zl == 4)
+
+    def near_chunk(i):
+        return h * 4 + mid + (near(i, mid, 4) if i else 0)
+
+    def far_chunk(i):
+        step = near(i, mid, 4) if i else 0
+        if i in (1, 2):
+            step = jnp.where(swap, near(3 - i, mid, 4), step)
+        return (1 - h) * 4 + mid + step
+
+    def arrive(q):
+        for k in range(2):
+            wait(rows((2 * q + k) * GROUP, GROUP), zsem.at[2 * q + k])
+
+    def forward():
+        with jax.named_scope("relay"):
+            for part in range(2):
+                wait(relay.at[pl.ds(part * 2 * BLOCK, 2 * BLOCK)], rsem.at[part])
+                onward(2 * part)
+                onward(2 * part + 1)
+
+    for i in range(7):
+        take(i)
+        if i:
+            with jax.named_scope(f"pass{i - 1}"):
+                pass_on(i - 1)
+    with jax.named_scope("pass6"):
+        pass_on(6)
+        for i in range(7):
+            from_core(i)
+
+    ahead = [near_chunk(i) for i in range(3)] + [far_chunk(3), far_chunk(2)]
+    upper = jnp.where(zl >= 4, 1, 0)
+    for slot, q in enumerate(ahead):
+        with jax.named_scope(f"ahead{slot}"):
+            if slot >= 3:
+                arrive(q)
+            left(q, upper * 4, 28, ahi, alo)
+            right(q, slot, bhi, blo)
+            multiply(slot, upper * 64, (224, 224), ahi, alo, bhi, blo, slot == 0)
+    with jax.named_scope("core"):
+        far_at = place(7)
+
+        def piece(base, dx):
+            return rows(base + far_at * GROUP + lax.rem(x - dx + 4, 4) * BLOCK, BLOCK)
+
+        for dx in range(4):
+            with jax.named_scope(f"own7{dx}"):
+                src = piece(h * HALF, dx)
+                wait(src, zsem.at[16 + lax.rem(x - dx + 4, 4)])
+            for dy in (1, 3, 2):
+                send(
+                    src,
+                    piece(ROW + r * HALF, dx),
+                    ysend,
+                    ysem.at[24 + dy * 4 + dx],
+                    device(0, dy, 0, 0),
+                )
+            to = device(0, 0, 0, 1)
+            send(src, piece(ROW + r * HALF, dx), csend, csem.at[32 + dx], to)
+        forward()
+        for dx in range(4):
+            for dy in (1, 3, 2):
+                ref = piece(ROW + (lax.rem(y - dy + 4, 4) * 2 + c) * HALF, dx)
+                wait(ref, ysem.at[24 + dy * 4 + dx])
+                send(ref, ref, csend, csem.at[32 + dy * 4 + dx], device(0, 0, 0, 1))
+        for dx in range(4):
+            for dy in (0, 1, 3, 2):
+                q = lax.rem(y - dy + 4, 4) * 2 + 1 - c
+                wait(piece(ROW + q * HALF, dx), csem.at[32 + dy * 4 + dx])
+    with jax.named_scope("near3"):
+        q = near_chunk(3)
+        left(q, upper * 4, 28, ahi, alo)
+        right(q, 5, bhi, blo)
+        multiply(5, upper * 64, (224, 224), ahi, alo, bhi, blo)
+    last = (1 - upper) * 28
+    for slot, q in enumerate([*ahead, near_chunk(3)]):
+        with jax.named_scope(f"late{slot}"):
+            left(q, last, 4, ahi, alo)
+            multiply(slot, last * 16, (64,), ahi, alo, bhi, blo, slot == 0)
+    ends = ((1, ahi, alo), (0, nhi, nlo))
+    for i, hi, lo in ends:
+        with jax.named_scope(f"left{i}"):
+            left(far_chunk(i), 0, 32, hi, lo)
+    for i, hi, lo in ends:
         with jax.named_scope(f"wait{i}"):
-            for k in range(2):
-                wait(rows((2 * q + k) * GROUP, GROUP), zsem.at[2 * q + k])
+            arrive(far_chunk(i))
         with jax.named_scope(f"far{i}"):
-            chunk(q, False)
-            multiply(False)
+            right(far_chunk(i), 0, whi, wlo)
+            multiply(0, 0, (256, 256), hi, lo, whi, wlo)
     with jax.named_scope("end"):
         wait(big.at[pl.ds(0, 63 * BLOCK)], zsend)
+        wait(big.at[pl.ds(0, 4 * BLOCK)], rsend)
         wait(big.at[pl.ds(0, 3 * HALF)], ysend)
         wait(big.at[pl.ds(0, 4 * HALF)], csend)
 
@@ -269,29 +389,41 @@
         kernel,
         name="multiples",
         out_shape=jax.ShapeDtypeStruct((2, FPD, N // 2, 128), jnp.float32),
-        in_specs=[pl.BlockSpec(memory_space=pltpu.HBM), vmem],
+        in_specs=[pl.BlockSpec(memory_space=pltpu.HBM)] * 2,
         out_specs=vmem,
         scratch_shapes=[
             pltpu.VMEM((2048, NT), jnp.float32),
+            pltpu.VMEM((2, 2 * NF, NT), jnp.bfloat16),
             pltpu.VMEM((2 * NF * 16, 128), jnp.float32),
             pltpu.VMEM((ROW + 8 * HALF, 128), jnp.float32),
             pltpu.VMEM((FPD, 512, 256), jnp.bfloat16),
             pltpu.VMEM((FPD, 512, 256), jnp.bfloat16),
+            pltpu.VMEM((6 * FPD, 256, 256), jnp.bfloat16),
+            pltpu.VMEM((6 * FPD, 256, 256), jnp.bfloat16),
             pltpu.VMEM((FPD, 256, 256), jnp.bfloat16),
             pltpu.VMEM((FPD, 256, 256), jnp.bfloat16),
-            dma((XPART,)),
+            pltpu.VMEM((FPD, 512, 256), jnp.bfloat16),
+            pltpu.VMEM((FPD, 512, 256), jnp.bfloat16),
+            dma((XPART + 1,)),
             dma,
             dma,
             dma,
             dma,
-            dma((16,)),
-            dma((24,)),
-            dma((32,)),
+            dma((20,)),
+            dma((40,)),
+            dma((48,)),
+            pltpu.SemaphoreType.REGULAR((2, 8)),
+            pltpu.VMEM((4 * BLOCK, 128), jnp.float32),
+            dma((2,)),
+            dma,
         ],
         compiler_params=pltpu.CompilerParams(
-            collective_id=0, has_side_effects=True, vmem_limit_bytes=40 << 20
+            collective_id=0, has_side_effects=True, vmem_limit_bytes=48 << 20
         ),
-    )(traces.reshape(2048, NT), table)
+    )(
+        pltpu.with_memory_space_constraint(traces.reshape(2048, NT), pltpu.HBM),
+        pltpu.with_memory_space_constraint(table, pltpu.HBM),
+    )
 
 
 def solution(mesh):

time: 165 us -> 155 us (0.939)
  the two profiles are of different devices: /device:TPU:1 before, /device:TPU:72 now
where the time goes in v2:
time: 155 us
  Pallas kernels  154 us (99%)
    pallas_call x1, Pallas kernels, per_device(): pl.pallas_call(kernel, name='multiples', out_shape=jax.ShapeDtypeStruct((...  154 us

profile of v2, /device:TPU:72, one launch (start us, length us, event | category | flops | bytes accessed | tf_op | source)
XLA Modules:
  0.0 155.3 jit_solution(6044041175286860193)
XLA Ops:
  0.0 154.1 %multiples.1 = f32[2,3,512,128]{3,2,1,0:T(8,128)S(1)} custom-call(f32[2048,256]{1,0:T(8,128)} %bitcast.1, bf16[2,192,256]{2,1,0:T(8,128)(2,1)} %constant.2.clone.table), custom_call_target="tpu_custom_call" | custom-call | tf_op jit(solution)/shard_map/multiples/pallas_call | solution.py:388
  154.2 1.1 copy.4

commit v3 on v2

--- a/solution.py
+++ b/solution.py
@@ -164,20 +164,20 @@
             zcopy(dz, dx)
 
     def via(dx):
-        return 4 if dx < 2 else -4
+        return 4 if dx % 2 == 0 else -4
 
     def halfway(dx):
         to = device(dx, 0, via(dx), 0)
         goal = device(dx, 0, 8, 0)[0]
         src = spec.at[pl.ds(pl.multiple_of(goal * BLOCK, BLOCK), BLOCK)]
-        slot = relay.at[pl.ds(dx * BLOCK, BLOCK)]
-        send(src, slot, zsend, rsem.at[dx // 2], to)
+        slot = relay.at[pl.ds((dx % 2 * 2 + dx // 2) * BLOCK, BLOCK)]
+        send(src, slot, zsend, rsem.at[dx % 2], to)
 
     def onward(dx):
         to = device(0, 0, via(dx), 0)
         first = lax.rem(z - via(dx) + 16, 16)
         block = (first * 4 + lax.rem(x - dx + 4, 4)) * BLOCK
-        slot = relay.at[pl.ds(dx * BLOCK, BLOCK)]
+        slot = relay.at[pl.ds((dx % 2 * 2 + dx // 2) * BLOCK, BLOCK)]
         send(slot, rows(block, BLOCK), rsend, zsem.at[first], to)
 
     for k in range(1, 8):
@@ -292,6 +292,8 @@
         step = near(i, mid, 4) if i else 0
         if i in (1, 2):
             step = jnp.where(swap, near(3 - i, mid, 4), step)
+        if i < 2:
+            step = jnp.where(zl == 2, 0 if i else near(2, mid, 4), step)
         return (1 - h) * 4 + mid + step
 
     def arrive(q):
@@ -302,8 +304,8 @@
         with jax.named_scope("relay"):
             for part in range(2):
                 wait(relay.at[pl.ds(part * 2 * BLOCK, 2 * BLOCK)], rsem.at[part])
-                onward(2 * part)
-                onward(2 * part + 1)
+                onward(part)
+                onward(part + 2)
 
     for i in range(7):
         take(i)

time: 155 us -> 154 us (level)
  the two profiles are of different devices: /device:TPU:72 before, /device:TPU:64 now
where the time goes in v3:
time: 154 us
  Pallas kernels  153 us (99%)
    pallas_call x1, Pallas kernels, per_device(): pl.pallas_call(kernel, name='multiples', out_shape=jax.ShapeDtypeStruct((...  153 us

profile of v3, /device:TPU:64, one launch (start us, length us, event | category | flops | bytes accessed | tf_op | source)
XLA Modules:
  0.0 154.4 jit_solution(12886873781506650806)
XLA Ops:
  0.0 153.2 %multiples.1 = f32[2,3,512,128]{3,2,1,0:T(8,128)S(1)} custom-call(f32[2048,256]{1,0:T(8,128)} %bitcast.1, bf16[2,192,256]{2,1,0:T(8,128)(2,1)} %constant.2.clone.table), custom_call_target="tpu_custom_call" | custom-call | tf_op jit(solution)/shard_map/multiples/pallas_call | solution.py:390
  153.2 1.1 copy.4

commit v4 on v3

--- a/solution.py
+++ b/solution.py
@@ -375,7 +375,7 @@
             arrive(far_chunk(i))
         with jax.named_scope(f"far{i}"):
             right(far_chunk(i), 0, whi, wlo)
-            multiply(0, 0, (256, 256), hi, lo, whi, wlo)
+            multiply(0, 0, (512,), hi, lo, whi, wlo)
     with jax.named_scope("end"):
         wait(big.at[pl.ds(0, 63 * BLOCK)], zsend)
         wait(big.at[pl.ds(0, 4 * BLOCK)], rsend)

time: 154 us -> 154 us (level)
  no operation moved by 1% of the time
where the time goes in v4:
time: 154 us
  Pallas kernels  153 us (99%)
    pallas_call x1, Pallas kernels, per_device(): pl.pallas_call(kernel, name='multiples', out_shape=jax.ShapeDtypeStruct((...  153 us

profile of v4, /device:TPU:64, one launch (start us, length us, event | category | flops | bytes accessed | tf_op | source)
XLA Modules:
  0.0 154.3 jit_solution(5450676093560396605)
XLA Ops:
  0.0 153.2 %multiples.1 = f32[2,3,512,128]{3,2,1,0:T(8,128)S(1)} custom-call(f32[2048,256]{1,0:T(8,128)} %bitcast.1, bf16[2,192,256]{2,1,0:T(8,128)(2,1)} %constant.2.clone.table), custom_call_target="tpu_custom_call" | custom-call | tf_op jit(solution)/shard_map/multiples/pallas_call | solution.py:390
  153.2 1.1 copy.4
